TPU v7x, 32 devices: a whole 2x2x4 slice. The times are simulated.
32 devices in a mesh: row: 8 (over z, core), col: 4 (over y, x).
Axes of the slice: x: 2, y: 2, z: 4, core: 2. Of those that a mesh axis runs over, the one named last changes fastest.
Arguments:
- similarity: bfloat16 [2048, 2048], P('row', 'col')
- in_mask: int32 [8, 8], P('row', 'col'), may hold values from 0 to 1, as said below
- out_mask: int32 [8, 8], P('row', 'col'), may hold values from 0 to 1, as said below
Outputs:
- stochastic: float32 [2048, 2048], P('row', 'col')
Inputs may be any that keep to these rules, and one draw needn't show every extreme that they name: in_mask is symmetric, similarity is symmetric and nonnegative with positive diagonal entries, and every diagonal block is present. `out_mask`: every diagonal block is kept.
All inputs are finite; a program needn't handle non-finite values.
Results may differ from a plain program's by a relative error of at most 0.0003.
Values may be sent and summed in bfloat16 or wider, within the bound.
No kernel may reach another device: no remote copies, remote signals or barrier semaphores. Data moves between devices by JAX's collectives and lax.ppermute only.
A program may use at most 64 MiB of HBM per device.

v0:
```python
import jax
import jax.numpy as jnp
from jax import lax
from jax.sharding import PartitionSpec as P

BS = 256


def on_device(similarity, in_mask, out_mask):
    rows_loc, cols_loc = similarity.shape
    rblocks, cblocks = in_mask.shape
    live = in_mask.astype(jnp.bfloat16)[:, None, :, None]
    sparse = (similarity.reshape(rblocks, BS, cblocks, BS) * live).reshape(rows_loc, cols_loc)
    row_panel = lax.all_gather(sparse, "col", axis=1, tiled=True)
    product = jnp.dot(
        row_panel,
        lax.all_gather(sparse, "row", axis=0, tiled=True),
        preferred_element_type=jnp.float32,
    )
    keep = out_mask.astype(jnp.float32)[:, None, :, None]
    kept = (product.reshape(rblocks, BS, cblocks, BS) * keep).reshape(rows_loc, cols_loc)
    inflated = kept * kept
    column_sums = lax.psum(jnp.sum(inflated, axis=0), "row")
    total = jnp.float32(rows_loc * lax.axis_size("row"))
    return inflated * (total / column_sums)[None, :]


def solution(mesh):
    in_specs = (P("row", "col"), P("row", "col"), P("row", "col"))
    out_specs = P("row", "col")
    return jax.shard_map(
        on_device, mesh=mesh, in_specs=in_specs, out_specs=out_specs, check_vma=False
    )
```

profile of v0, /device:TPU:0, one launch (start us, length us, event | category | flops | bytes accessed | tf_op | source)
XLA Modules:
  0.0 94.9 jit_solution(12435030798267104924)
XLA Ops:
  6.5 0.0 all-gather.3.cloned.1.call-start
  6.5 0.7 convert_bitcast_fusion.1
  7.2 0.1 broadcast_bitcast_fusion.1
  7.3 1.7 %broadcast_multiply_fusion.1 = bf16[256,512]{1,0:T(8,128)(2,1)} fusion(bf16[256,512]{1,0:T(8,128)(2,1)} %param.3, bf16[512]{0:T(512)(128)(2,1)S(1)} %bitcast.12), kind=kLoop, calls=%fused_computation.3 | loop fusion | flops 131072 | bytes 525312 | tf_op jit(solution)/shard_map/mul | solution.py:13
  9.0 0.0 all-gather.3.cloned.1.call-update
  9.0 0.0 all-gather.5.cloned.1.call-start
  9.0 0.7 all-gather.5.cloned.1.call-update
  9.7 0.7 convert_bitcast_fusion
  10.4 0.1 broadcast_bitcast_fusion
  10.5 27.9 %all-gather.3.cloned.1.call-done = bf16[256,2048]{1,0:T(8,128)(2,1)} async-done(((bf16[256,512]{1,0:T(8,128)(2,1)}), bf16[256,2048]{1,0:T(8,128)(2,1)}) %all-gather.3.cloned.1.call-update) | async-done | bytes 1048592 | tf_op jit(solution)/shard_map/all_gather | solution.py:14
  38.4 30.7 %all-gather.5.cloned.1.call-done = bf16[2048,512]{1,0:T(8,128)(2,1)} async-done(((bf16[256,512]{1,0:T(8,128)(2,1)}), bf16[2048,512]{1,0:T(8,128)(2,1)}) %all-gather.5.cloned.1.call-update) | async-done | bytes 2097168 | tf_op jit(solution)/shard_map/all_gather | solution.py:17
  69.1 2.6 %fusion.1 = (f32[512]{0:T(512)S(1)}, f32[256,512]{1,0:T(8,128)S(1)}) fusion(f32[512]{0:T(512)S(1)} %bitcast.13, bf16[256,2048]{1,0:T(8,128)(2,1)} %all-gather.3.cloned.1.call-done, bf16[2048,512]{1,0:T(8,128)(2,1)} %all-gather.5.cloned.1.call-done), kind=kOutput, calls=%fused_computation.9 | convolution fusion | flops 537263616 | bytes 3674112 | tf_op jit(solution)/shard_map/dot_general | solution.py:15
  71.8 15.4 %psum.7 = f32[512]{0:T(512)S(1)} all-reduce(f32[512]{0:T(512)S(1)} %get-tuple-element.5), channel_id=1, replica_groups=mesh['row'=8,'col'=4] {'row'}, use_global_device_ids=true, to_apply=%region_1.0 | all-reduce | flops 512 | bytes 4096 | tf_op jit(solution)/shard_map/psum | solution.py:23
  87.2 0.9 broadcast_multiply_fusion
  (3 shorter events, 0.0 us)
Async XLA Ops:
  6.5 31.9 %all-gather.3.cloned.1.call-start = ((), (), s32[]{:S(2)}) async-start(), calls=%async_computation | async-start | bytes 1310720 | tf_op jit(solution)/shard_map/all_gather | solution.py:14
  9.0 60.2 %all-gather.5.cloned.1.call-start = ((), (), s32[]{:S(2)}) async-start(), calls=%async_computation.1 | async-start | bytes 2359296 | tf_op jit(solution)/shard_map/all_gather | solution.py:17
Sparse Core Ops, SparseCore 0:
  9.2 29.1 all-gather.2
  40.0 29.0 all-gather.4
where the time goes:
time: 95.1 us; the launch traced here: 94.9 us
  waiting for transfers between devices  59.4 us (62%)
  blocking collectives  15.4 us (16%)
  between operations  13.4 us (14%)
  other arithmetic  3.87 us (4%)
  matrix products  2.64 us (3%)
    all_gather x1, waiting for transfers between devices, on_device(): lax.all_gather(sparse, 'row', axis=0, tiled=True)  30.7 us
    all_gather x1, waiting for transfers between devices, on_device(): row_panel = lax.all_gather(sparse, 'col', axis=1, tiled=True)  27.9 us
    psum x1, blocking collectives, on_device(): column_sums = lax.psum(jnp.sum(inflated, axis=0), 'row')  15.4 us
    dot_general x1, matrix products, on_device(): jnp.dot(row_panel, lax.all_gather(sparse, 'row', axis=0, tiled=True), pre...  2.64 us
    mul x2, other arithmetic, on_device(): similarity.reshape(rblocks, BS, cblocks, BS) * live  2.33 us
  transfers between devices with their start and end apart: 2, of which 2 were waited for; matrix products, arithmetic and copies ran while one was open for 1% of the time, Pallas kernels for 0%

commit v1 on v0

--- a/solution.py
+++ b/solution.py
@@ -2,6 +2,7 @@
 import jax.numpy as jnp
 from jax import lax
 from jax.sharding import PartitionSpec as P
+from jax.lax import axis_index, axis_size, ppermute
 
 BS = 256
 
@@ -12,11 +13,23 @@
     live = in_mask.astype(jnp.bfloat16)[:, None, :, None]
     sparse = (similarity.reshape(rblocks, BS, cblocks, BS) * live).reshape(rows_loc, cols_loc)
     row_panel = lax.all_gather(sparse, "col", axis=1, tiled=True)
-    product = jnp.dot(
-        row_panel,
-        lax.all_gather(sparse, "row", axis=0, tiled=True),
-        preferred_element_type=jnp.float32,
-    )
+
+    def search_shelves(t0):
+        q_n = axis_size("row")
+        copies = [(kk, (kk + 1) % q_n) for kk in range(q_n)]
+        all_blocks = [(kk, (kk - 1) % q_n) for kk in range(q_n)]
+        passed, even = ([t0], [t0])
+        for _ in range(q_n // 2):
+            passed.append(ppermute(passed[-1], "row", perm=copies))
+        for _ in range((q_n - 1) // 2):
+            even.append(ppermute(even[-1], axis_name="row", perm=all_blocks))
+        return jnp.roll(
+            jnp.concatenate([*passed[::-1], *even[1:]], axis=0),
+            (axis_index("row") - q_n // 2) * t0.shape[0],
+            axis=0,
+        )
+
+    product = jnp.dot(row_panel, search_shelves(sparse), preferred_element_type=jnp.float32)
     keep = out_mask.astype(jnp.float32)[:, None, :, None]
     kept = (product.reshape(rblocks, BS, cblocks, BS) * keep).reshape(rows_loc, cols_loc)
     inflated = kept * kept

time: 95.1 us -> 82.3 us (0.87)
  waiting for transfers between devices: 59.4 us -> 24.2 us
  starting transfers between devices: 0.04 us -> 11.2 us
  local copies, waits for them, and re-layouts: 0.16 us -> 10.2 us
  other arithmetic: 3.87 us -> 5.66 us
    all_gather x1 -> x0, waiting for transfers between devices: 30.7 us -> none  [on_device(): lax.all_gather(sparse, 'row', axis=0, tiled=True)]
    all_gather x1, waiting for transfers between devices: 27.9 us -> 0.01 us  [on_device(): row_panel = lax.all_gather(sparse, 'col', axis=1, tiled=True)]
    ppermute x0 -> x7, waiting for transfers between devices: none -> 24.1 us  [the longest x4 24.1 us: search_shelves(): passed.append(ppermute(passed[-1], 'row', perm=copies))]
    ppermute x0 -> x7, starting transfers between devices: none -> 11.2 us  [the longest x3 10.7 us: search_shelves(): even.append(ppermute(even[-1], axis_name='row', perm=all_blocks))]
    unnamed x4 -> x21, local copies, waits for them, and re-layouts: 0.16 us -> 9.45 us
    unnamed x0 -> x2, other arithmetic: none -> 2.45 us
  transfers between devices with their start and end apart: 2 -> 8, of which waited for: 2 -> 4; matrix products, arithmetic and copies ran while one was open for 1% -> 16% of each run, Pallas kernels for 0% -> 0%
where the time goes in v1:
time: 82.3 us; the launch traced here: 82.1 us
  waiting for transfers between devices  24.2 us (29%)
  blocking collectives  14.9 us (18%)
  between operations  13.4 us (16%)
  starting transfers between devices  11.2 us (14%)
  local copies, waits for them, and re-layouts  10.2 us (12%)
  other arithmetic  5.66 us (7%)
  matrix products  2.64 us (3%)
    ppermute x4, waiting for transfers between devices, search_shelves(): passed.append(ppermute(passed[-1], 'row', perm=copies))  24.1 us
    psum x1, blocking collectives, on_device(): column_sums = lax.psum(jnp.sum(inflated, axis=0), 'row')  14.9 us
    ppermute x3, starting transfers between devices, search_shelves(): even.append(ppermute(even[-1], axis_name='row', perm=all_blocks))  10.7 us
    unnamed x21, local copies, waits for them, and re-layouts  9.45 us
    dot_general x1, matrix products, on_device(): jnp.dot(row_panel, search_shelves(sparse), preferred_element_type=jnp.flo...  2.64 us
    unnamed x2, other arithmetic  2.45 us
    mul x2, other arithmetic, on_device(): similarity.reshape(rblocks, BS, cblocks, BS) * live  1.67 us
  transfers between devices with their start and end apart: 8, of which 4 were waited for; matrix products, arithmetic and copies ran while one was open for 16% of the time, Pallas kernels for 0%

profile of v1, /device:TPU:0, one launch (start us, length us, event | category | flops | bytes accessed | tf_op | source)
XLA Modules:
  0.0 82.1 jit_solution(11573594308289691060)
XLA Ops:
  7.3 1.0 %broadcast_multiply_fusion.1 = bf16[256,512]{1,0:T(8,128)(2,1)S(1)} fusion(bf16[256,512]{1,0:T(8,128)(2,1)} %param.3, bf16[512]{0:T(512)(128)(2,1)S(1)} %bitcast.11), kind=kLoop, calls=%fused_computation.5 | loop fusion | flops 131072 | bytes 525312 | tf_op jit(solution)/shard_map/mul | solution.py:14
  8.8 8.1 %collective-permute-done = bf16[256,512]{1,0:T(8,128)(2,1)S(1)} collective-permute-done((bf16[256,512]{1,0:T(8,128)(2,1)S(1)}, bf16[256,512]{1,0:T(8,128)(2,1)S(1)}, u32[]{:S(2)}, u32[]{:S(2)}) %collective-permute-start) | collective-permute-done | bytes 262176 | tf_op jit(solution)/shard_map/ppermute | solution.py:23
  16.9 3.5 %collective-permute-start.4 = (bf16[256,512]{1,0:T(8,128)(2,1)S(1)}, bf16[256,512]{1,0:T(8,128)(2,1)S(1)}, u32[]{:S(2)}, u32[]{:S(2)}) collective-permute-start(bf16[256,512]{1,0:T(8,128)(2,1)S(1)} %broadcast_multiply_fusion.1), channel_id=1, source_target_pairs={{0,28},{4,0},{8,4},{12,8},{16,12},{20,16},{24,20},{28,24},{1,29},{... | collective-permute-start | bytes 786440 | tf_op jit(solution)/shard_map/ppermute | solution.py:25
  20.5 6.1 %collective-permute-done.1 = bf16[256,512]{1,0:T(8,128)(2,1)S(1)} collective-permute-done((bf16[256,512]{1,0:T(8,128)(2,1)S(1)}, bf16[256,512]{1,0:T(8,128)(2,1)S(1)}, u32[]{:S(2)}, u32[]{:S(2)}) %collective-permute-start.1) | collective-permute-done | bytes 262176 | tf_op jit(solution)/shard_map/ppermute | solution.py:23
  26.6 3.6 %collective-permute-start.5 = (bf16[256,512]{1,0:T(8,128)(2,1)S(1)}, bf16[256,512]{1,0:T(8,128)(2,1)S(1)}, u32[]{:S(2)}, u32[]{:S(2)}) collective-permute-start(bf16[256,512]{1,0:T(8,128)(2,1)S(1)} %collective-permute-done.4), channel_id=1, source_target_pairs={{0,28},{4,0},{8,4},{12,8},{16,12},{20,16},{24,20},{28,24},{1,29},{... | collective-permute-start | bytes 786440 | tf_op jit(solution)/shard_map/ppermute | solution.py:25
  30.2 6.1 %collective-permute-done.2 = bf16[256,512]{1,0:T(8,128)(2,1)S(1)} collective-permute-done((bf16[256,512]{1,0:T(8,128)(2,1)S(1)}, bf16[256,512]{1,0:T(8,128)(2,1)S(1)}, u32[]{:S(2)}, u32[]{:S(2)}) %collective-permute-start.2) | collective-permute-done | bytes 262176 | tf_op jit(solution)/shard_map/ppermute | solution.py:23
  37.0 3.5 %collective-permute-start.6 = (bf16[256,512]{1,0:T(8,128)(2,1)S(1)}, bf16[256,512]{1,0:T(8,128)(2,1)S(1)}, u32[]{:S(2)}, u32[]{:S(2)}) collective-permute-start(bf16[256,512]{1,0:T(8,128)(2,1)S(1)} %collective-permute-done.5), channel_id=1, source_target_pairs={{0,28},{4,0},{8,4},{12,8},{16,12},{20,16},{24,20},{28,24},{1,29},{... | collective-permute-start | bytes 786440 | tf_op jit(solution)/shard_map/ppermute | solution.py:25
  40.6 3.9 %collective-permute-done.3 = bf16[256,512]{1,0:T(8,128)(2,1)S(1)} collective-permute-done((bf16[256,512]{1,0:T(8,128)(2,1)S(1)}, bf16[256,512]{1,0:T(8,128)(2,1)S(1)}, u32[]{:S(2)}, u32[]{:S(2)}) %collective-permute-start.3) | collective-permute-done | bytes 262176 | tf_op jit(solution)/shard_map/ppermute | solution.py:23
  44.4 0.7 constant_dynamic-update-slice_fusion.15
  45.1 0.7 constant_dynamic-update-slice_fusion.14
  45.8 0.7 constant_dynamic-update-slice_fusion.13
  46.6 0.7 constant_dynamic-update-slice_fusion.12
  47.3 1.7 %constant_dynamic-update-slice_fusion.11 = bf16[4096,512]{1,0:T(8,128)(2,1)} fusion(bf16[4096,512]{1,0:T(8,128)(2,1)} %constant_dynamic-update-slice_fusion.12, bf16[256,512]{1,0:T(8,128)(2,1)} %param.3, bf16[512]{0:T(512)(128)(2,1)S(1)} %bitcast.12), kind=kLoop, calls=%fused_computation.17 | loop fusion | flops 524288 | bytes 525312
  49.0 0.7 constant_dynamic-update-slice_fusion.10
  50.4 0.7 constant_dynamic-update-slice_fusion.8
  51.1 0.7 constant_dynamic-update-slice_fusion.7
  51.8 0.7 constant_dynamic-update-slice_fusion.6
  52.5 0.7 constant_dynamic-update-slice_fusion.5
  53.3 0.7 constant_dynamic-update-slice_fusion.4
  54.0 0.7 constant_dynamic-update-slice_fusion.3
  55.5 0.7 constant_dynamic-update-slice_fusion.1
  56.9 2.6 %fusion.9 = (f32[512]{0:T(512)S(1)}, f32[256,512]{1,0:T(8,128)S(1)}) fusion(f32[512]{0:T(512)S(1)} %bitcast.14, bf16[256,2048]{1,0:T(8,128)(2,1)} %all-gather.2.cloned.1.call-done, bf16[4096,512]{1,0:T(8,128)(2,1)} %constant_dynamic-update-slice_fusion, s32[]{:T(128)S(6)} %select_n.14), kind=kOutput, calls=%fused_computation.28 | convolution fusion | flops 537263616 | bytes 3674116 | tf_op jit(solution)/shard_map/dot_general | solution.py:32
  59.5 14.9 %psum.7 = f32[512]{0:T(512)S(1)} all-reduce(f32[512]{0:T(512)S(1)} %get-tuple-element.5), channel_id=1, replica_groups=mesh['row'=8,'col'=4] {'row'}, use_global_device_ids=true, to_apply=%region_1.2 | all-reduce | flops 512 | bytes 4096 | tf_op jit(solution)/shard_map/psum | solution.py:36
  74.4 0.9 %broadcast_multiply_fusion = f32[256,512]{1,0:T(8,128)} fusion(f32[256,512]{1,0:T(8,128)S(1)} %get-tuple-element.6, f32[512]{0:T(512)S(1)} %broadcast_divide_fusion), kind=kLoop, calls=%fused_computation.4 | loop fusion | flops 131072 | bytes 1050624 | tf_op jit(solution)/shard_map/mul | solution.py:38
  (24 shorter events, 4.2 us)
Async XLA Ops:
  6.5 47.5 %copy-start = (bf16[256,512]{1,0:T(8,128)(2,1)S(1)}, bf16[256,512]{1,0:T(8,128)(2,1)}, u32[]{:S(2)}) copy-start(bf16[256,512]{1,0:T(8,128)(2,1)} %param.3) | copy-start | bytes 786436
  6.5 50.3 %all-gather.2.cloned.1.call-start = ((), (), s32[]{:S(2)}) async-start(), calls=%async_computation | async-start | bytes 1310720 | tf_op jit(solution)/shard_map/all_gather | solution.py:15
  8.3 18.3 %copy-start.1 = (bf16[256,512]{1,0:T(8,128)(2,1)}, bf16[256,512]{1,0:T(8,128)(2,1)S(1)}, u32[]{:S(2)}) copy-start(bf16[256,512]{1,0:T(8,128)(2,1)S(1)} %broadcast_multiply_fusion.1) | copy-start | bytes 786436
  8.3 8.6 %collective-permute-start = (bf16[256,512]{1,0:T(8,128)(2,1)S(1)}, bf16[256,512]{1,0:T(8,128)(2,1)S(1)}, u32[]{:S(2)}, u32[]{:S(2)}) collective-permute-start(bf16[256,512]{1,0:T(8,128)(2,1)S(1)} %broadcast_multiply_fusion.1), channel_id=1, source_target_pairs={{0,4},{4,8},{8,12},{12,16},{16,20},{20,24},{24,28},{28,0},{1,5},{5... | collective-permute-start | bytes 786440 | tf_op jit(solution)/shard_map/ppermute | solution.py:23
  16.9 9.6 %collective-permute-start.1 = (bf16[256,512]{1,0:T(8,128)(2,1)S(1)}, bf16[256,512]{1,0:T(8,128)(2,1)S(1)}, u32[]{:S(2)}, u32[]{:S(2)}) collective-permute-start(bf16[256,512]{1,0:T(8,128)(2,1)S(1)} %collective-permute-done), channel_id=1, source_target_pairs={{0,4},{4,8},{8,12},{12,16},{16,20},{20,24},{24,28},{28,0},{1,5},{5... | collective-permute-start | bytes 786440 | tf_op jit(solution)/shard_map/ppermute | solution.py:23
  16.9 9.7 %collective-permute-start.4 = (bf16[256,512]{1,0:T(8,128)(2,1)S(1)}, bf16[256,512]{1,0:T(8,128)(2,1)S(1)}, u32[]{:S(2)}, u32[]{:S(2)}) collective-permute-start(bf16[256,512]{1,0:T(8,128)(2,1)S(1)} %broadcast_multiply_fusion.1), channel_id=1, source_target_pairs={{0,28},{4,0},{8,4},{12,8},{16,12},{20,16},{24,20},{28,24},{1,29},{... | collective-permute-start | bytes 786440 | tf_op jit(solution)/shard_map/ppermute | solution.py:25
  26.5 9.7 %collective-permute-start.2 = (bf16[256,512]{1,0:T(8,128)(2,1)S(1)}, bf16[256,512]{1,0:T(8,128)(2,1)S(1)}, u32[]{:S(2)}, u32[]{:S(2)}) collective-permute-start(bf16[256,512]{1,0:T(8,128)(2,1)S(1)} %collective-permute-done.1), channel_id=1, source_target_pairs={{0,4},{4,8},{8,12},{12,16},{16,20},{20,24},{24,28},{28,0},{1,5},{5... | collective-permute-start | bytes 786440 | tf_op jit(solution)/shard_map/ppermute | solution.py:23
  26.6 10.4 %collective-permute-start.5 = (bf16[256,512]{1,0:T(8,128)(2,1)S(1)}, bf16[256,512]{1,0:T(8,128)(2,1)S(1)}, u32[]{:S(2)}, u32[]{:S(2)}) collective-permute-start(bf16[256,512]{1,0:T(8,128)(2,1)S(1)} %collective-permute-done.4), channel_id=1, source_target_pairs={{0,28},{4,0},{8,4},{12,8},{16,12},{20,16},{24,20},{28,24},{1,29},{... | collective-permute-start | bytes 786440 | tf_op jit(solution)/shard_map/ppermute | solution.py:25
  36.3 8.1 %collective-permute-start.3 = (bf16[256,512]{1,0:T(8,128)(2,1)S(1)}, bf16[256,512]{1,0:T(8,128)(2,1)S(1)}, u32[]{:S(2)}, u32[]{:S(2)}) collective-permute-start(bf16[256,512]{1,0:T(8,128)(2,1)S(1)} %collective-permute-done.2), channel_id=1, source_target_pairs={{0,4},{4,8},{8,12},{12,16},{16,20},{20,24},{24,28},{28,0},{1,5},{5... | collective-permute-start | bytes 786440 | tf_op jit(solution)/shard_map/ppermute | solution.py:23
  37.0 13.4 %collective-permute-start.6 = (bf16[256,512]{1,0:T(8,128)(2,1)S(1)}, bf16[256,512]{1,0:T(8,128)(2,1)S(1)}, u32[]{:S(2)}, u32[]{:S(2)}) collective-permute-start(bf16[256,512]{1,0:T(8,128)(2,1)S(1)} %collective-permute-done.5), channel_id=1, source_target_pairs={{0,28},{4,0},{8,4},{12,8},{16,12},{20,16},{24,20},{28,24},{1,29},{... | collective-permute-start | bytes 786440 | tf_op jit(solution)/shard_map/ppermute | solution.py:25
Sparse Core Ops, SparseCore 0:
  26.7 28.6 all-gather.1
